TPU v7x, 512 devices: a whole 4x4x16 slice. The times are simulated.
512 devices in a mesh: row: 16 (over y, x), col: 32 (over z, core).
Axes of the slice: x: 4, y: 4, z: 16, core: 2. Of those that a mesh axis runs over, the one named last changes fastest.
Arguments:
- div_blocks: float32 [1024, 6, 128, 128], P(('row', 'col')), may hold values from -0.5 to 0.5
- div_owner: int32 [1024, 6], P(('row', 'col')), may hold values from 0 to 15, as said below
- div_local: int32 [1024, 6], P(('row', 'col')), may hold values from 0 to 1
- div_count: int32 [1024], P(('row', 'col')), may hold values from 2 to 6
- inv_blocks: float32 [1024, 5, 128, 128], P(('row', 'col')), may hold values from -6 to 6
- inv_cols: int32 [1024, 5], P(('row', 'col')), may hold values from 0 to 5, as said below
- inv_count: int32 [1024], P(('row', 'col')), may hold values from 3 to 5
- schur_cols: int32 [1024, 4], P(('row', 'col')), may hold values from 0 to 1023, as said below
- schur_count: int32 [1024], P(('row', 'col')), may hold values from 2 to 4
Outputs:
- schur_blocks: float32 [1024, 4, 128, 128], P(('row', 'col'))
Inputs may be any that keep to these rules, and one draw needn't show every extreme that they name: `div_owner`: over all 6 slots of the 2 rows of one device, live or not, at most 2 name the same owner, and exactly 2 do for some owner on every device. `inv_cols`: the columns of one row are distinct. `schur_cols`: slot 0 of row p is p itself, slot 1 another row of the same subdomain, slot 2 a row of the subdomain with the same a and c + 1 mod 32, slot 3 one of the subdomain with c - 1 mod 32.
All inputs are finite; a program needn't handle non-finite values.
Results may differ from a plain program's by a relative error of at most 0.0003.
Values sent between devices are 32-bit elements; how exact they have to be, the bound alone decides.
A program may use at most 128 MiB of HBM per device.

v0:
```python
import jax
import jax.numpy as jnp
from jax import lax
from jax.sharding import PartitionSpec as P


def extended(block, sides, width):
    for axis, dim in sides:
        count = lax.axis_size(axis)
        forward = [(i, i + 1) for i in range(count - 1)]
        forward.append((count - 1, 0))
        backward = [(target, source) for source, target in forward]
        low = lax.ppermute(
            lax.slice_in_dim(block, block.shape[dim] - width, None, axis=dim), axis, forward
        )
        high = lax.ppermute(lax.slice_in_dim(block, 0, width, axis=dim), axis, backward)
        block = jnp.concatenate([low, block, high], axis=dim)
    return block


def local(
    div_blocks,
    div_owner,
    div_local,
    div_count,
    inv_blocks,
    inv_cols,
    inv_count,
    schur_cols,
    schur_count,
):
    rows_here = div_blocks.shape[0]
    slots_row = div_blocks.shape[1]
    block_side = div_blocks.shape[2]
    vel_here = inv_cols.shape[0]
    inv_slots = inv_cols.shape[1]
    pattern = schur_cols.shape[1]
    owner_count = lax.axis_size("row")
    lon_devices = lax.axis_size("col")
    listed = rows_here * slots_row
    capacity = max(2, -(-listed // owner_count))
    spaces = owner_count * capacity
    device = lax.axis_index("row") * lon_devices + lax.axis_index("col")
    press_ids = device * rows_here + jnp.arange(rows_here, dtype=jnp.int32)
    slot_live = jnp.arange(slots_row, dtype=jnp.int32)[None, :] < div_count[:, None]
    live_flat = slot_live.reshape(listed)
    target = div_owner.reshape(listed)
    positions = jnp.arange(listed, dtype=jnp.int32)
    before = (
        (positions[None, :] < positions[:, None])
        & live_flat[None, :]
        & (target[None, :] == target[:, None])
    )
    slot_rank = jnp.sum(before.astype(jnp.int32), axis=1)
    position = target * capacity + slot_rank
    placed = (position[:, None] == jnp.arange(spaces, dtype=jnp.int32)[None, :]) & live_flat[
        :, None
    ]
    placed_int = placed.astype(jnp.int32)
    source_slot = jnp.sum(placed_int * positions[:, None], axis=0)
    filled = jnp.sum(placed_int, axis=0) > 0
    flat_blocks = div_blocks.reshape(listed, block_side, block_side)
    outgoing = jnp.where(filled[:, None, None], jnp.take(flat_blocks, source_slot, axis=0), 0.0)
    pattern_live = jnp.arange(pattern, dtype=jnp.int32)[None, :] < schur_count[:, None]
    targets = jnp.where(pattern_live, schur_cols, -1)
    slot_meta = jnp.concatenate(
        [
            (div_local + 1)[:, :, None],
            jnp.broadcast_to(press_ids[:, None, None], (rows_here, slots_row, 1)),
            jnp.broadcast_to(targets[:, None, :], (rows_here, slots_row, pattern)),
        ],
        axis=2,
    ).reshape(listed, 2 + pattern)
    meta_out = jnp.sum(placed_int[:, :, None] * slot_meta[:, None, :], axis=0)
    arrived, meta_in = (
        lax.all_to_all(outgoing, "row", split_axis=0, concat_axis=0, tiled=True),
        lax.all_to_all(meta_out, "row", split_axis=0, concat_axis=0, tiled=True),
    )
    ext_blocks, ext_meta = (
        extended(arrived, (("col", 0),), spaces),
        extended(meta_in, (("col", 0),), spaces),
    )
    ext_cols = 3 * vel_here
    inv_live = jnp.arange(inv_slots, dtype=jnp.int32)[None, :] < inv_count[:, None]
    select_cols = (
        (inv_cols[:, :, None] == jnp.arange(ext_cols, dtype=jnp.int32)[None, None, :])
        & inv_live[:, :, None]
    ).astype(jnp.float32)
    dense_inv = jnp.einsum(
        "ukv,ukpq->uvpq", select_cols, inv_blocks, precision=lax.Precision.HIGHEST
    )
    own_live = meta_in[:, 0] > 0
    own_vel = meta_in[:, 0] - 1
    own_targets = meta_in[:, 2:]
    pick_rows = (own_vel[:, None] == jnp.arange(vel_here, dtype=jnp.int32)[None, :]) & own_live[
        :, None
    ]
    region_ids = jnp.arange(3 * spaces, dtype=jnp.int32) // spaces
    ext_live = ext_meta[:, 0] > 0
    column_index = region_ids * vel_here + jnp.maximum(ext_meta[:, 0] - 1, 0)
    chosen = jnp.take(dense_inv, column_index, axis=1)
    products = jnp.einsum("ugpq,grq->ugpr", chosen, ext_blocks, precision=lax.Precision.HIGHEST)
    matches = (
        (ext_meta[None, None, :, 1] == own_targets[:, :, None])
        & (own_targets[:, :, None] >= 0)
        & ext_live[None, None, :]
    )
    weight = (pick_rows[:, None, :, None] & matches[:, :, None, :]).astype(jnp.float32)
    factors = jnp.einsum("stug,ugpr->stpr", weight, products, precision=lax.Precision.HIGHEST)
    answer = jnp.einsum("spq,stqr->stpr", arrived, factors, precision=lax.Precision.HIGHEST)
    returned = lax.all_to_all(answer, "row", split_axis=0, concat_axis=0, tiled=True)
    taken = jnp.take(returned, position, axis=0)
    taken = jnp.where(live_flat[:, None, None, None], taken, 0.0)
    schur_blocks = jnp.sum(
        taken.reshape(rows_here, slots_row, pattern, block_side, block_side), axis=1
    )
    return schur_blocks


def solution(mesh):
    placed = (
        P(("row", "col"), None, None, None),
        P(("row", "col"), None),
        P(("row", "col"), None),
        P(("row", "col")),
        P(("row", "col"), None, None, None),
        P(("row", "col"), None),
        P(("row", "col")),
        P(("row", "col"), None),
        P(("row", "col")),
    )
    return jax.shard_map(
        local,
        mesh=mesh,
        in_specs=placed,
        out_specs=P(("row", "col"), None, None, None),
        check_vma=False,
    )
```

profile of v0, /device:TPU:97, one launch (start us, length us, event | category | flops | bytes accessed | tf_op | source)
XLA Modules:
  0.0 283.3 jit_solution(8411913473324732974)
XLA Ops:
  0.0 0.8 iota_compare_fusion.4
  0.8 0.1 lt.118
  0.9 0.8 reshape.282
  1.6 0.2 convert_reduce_fusion
  1.8 0.1 fusion.39
  2.0 0.1 copy.79
  2.0 0.1 fusion.29
  2.2 0.7 gather_fusion
  2.9 1.6 select_select_fusion
  4.5 6.9 %all-to-all-start.1 = ((f32[32,128,128]{2,1,0:T(8,128)}), f32[32,128,128]{2,1,0:T(8,128)S(1)}, u32[]{:S(2)}, u32[]{:S(2)}) async-start(f32[32,128,128]{2,1,0:T(8,128)} %select_select_fusion), calls=%async_computation.1 | async-start | bytes 4194304 | tf_op jit(solution)/shard_map/all_to_all | solution.py:76
  11.5 0.1 broadcast_in_dim.63
  11.6 0.1 concatenate.14
  11.8 0.1 copy.72
  11.9 0.1 broadcast_in_dim.102
  12.0 0.1 concatenate.15
  12.1 0.1 copy.73
  12.2 0.1 fusion.33
  12.2 29.7 %all-to-all-done.1 = f32[32,128,128]{2,1,0:T(8,128)S(1)} async-done(((f32[32,128,128]{2,1,0:T(8,128)}), f32[32,128,128]{2,1,0:T(8,128)S(1)}, u32[]{:S(2)}, u32[]{:S(2)}) %all-to-all-start.1) | async-done | bytes 2097184 | tf_op jit(solution)/shard_map/all_to_all | solution.py:76
  41.9 2.1 collective-permute-start.3
  44.1 2.7 collective-permute-start.2
  46.8 0.1 multiply_reduce_fusion
  46.9 0.7 copy.74
  47.6 3.5 %all-to-all-start = ((s32[16,2,6]{2,1,0:T(2,128)}), s32[16,2,6]{2,1,0:T(2,128)S(1)}, u32[]{:S(2)}, u32[]{:S(2)}) async-start(s32[16,2,6]{2,1,0:T(2,128)} %bitcast.1), calls=%async_computation | async-start | bytes 32768 | tf_op jit(solution)/shard_map/all_to_all | solution.py:77
  51.1 0.1 iota_compare_fusion.3
  51.2 0.9 fusion.23
  52.1 0.2 copy.83
  52.3 5.2 %all-to-all-done = s32[16,2,6]{2,1,0:T(2,128)S(1)} async-done(((s32[16,2,6]{2,1,0:T(2,128)}), s32[16,2,6]{2,1,0:T(2,128)S(1)}, u32[]{:S(2)}, u32[]{:S(2)}) %all-to-all-start) | async-done | bytes 800 | tf_op jit(solution)/shard_map/all_to_all | solution.py:77
  57.5 0.1 copy.76
  57.5 3.0 %collective-permute-start = (s32[32,6]{1,0:T(8,128)S(1)}, s32[32,6]{1,0:T(8,128)S(1)}, u32[]{:S(2)}, u32[]{:S(2)}) collective-permute-start(s32[32,6]{1,0:T(8,128)S(1)} %bitcast.65), channel_id=1, source_target_pairs={{0,1},{1,2},{2,3},{3,4},{4,5},{5,6},{6,7},{7,8},{8,9},{9,10},{10,1... | collective-permute-start | bytes 2312 | tf_op jit(solution)/shard_map/ppermute | solution.py:13
  60.5 0.1 compare_reduce_fusion
  60.6 0.1 add_reduce_fusion
  60.8 9.9 %collective-permute-done.1 = s32[32,6]{1,0:T(8,128)S(1)} collective-permute-done((s32[32,6]{1,0:T(8,128)S(1)}, s32[32,6]{1,0:T(8,128)S(1)}, u32[]{:S(2)}, u32[]{:S(2)}) %collective-permute-start.1) | collective-permute-done | bytes 800 | tf_op jit(solution)/shard_map/ppermute | solution.py:16
  70.7 0.1 copy.77
  70.8 0.1 copy.75
  70.8 0.1 pad_add_fusion
  71.0 8.6 %gather_fusion.1 = f32[96,2,128,128]{3,2,1,0:T(8,128)} fusion(f32[2,6,128,128]{3,2,1,0:T(8,128)S(1)} %copy.83, s32[1024]{0:T(1024)S(1)} %pad_clamp_fusion.1), kind=kCustom, calls=%fused_computation.1 | custom fusion | bytes 25166208 | tf_op jit(solution)/shard_map/jit(_take)/gather | solution.py:101
  79.6 0.1 and_and_fusion
  79.7 18.6 %fusion.13 = f32[2,96,128,128]{2,3,0,1:T(8,128)} fusion(f32[96,2,128,128]{3,2,1,0:T(8,128)} %gather_fusion.1, pred[96]{0:T(512)(128)(4,1)S(1)} %get-tuple-element.7, f32[32,128,128]{2,1,0:T(8,128)} %collective-permute-done.3, f32[32,128,128]{2,1,0:T(8,128)S(1)} %all-to-all-done.1, f32[32,128,128]{2,1,0:T(8,128)} %collective-permute-done.2), kind=kOutput, calls=%fused_computation.17 | convolution fusion | flops 4838129664 | bytes 31457376 | tf_op jit(solution)/shard_map/ugpq,grq->ugpr/dot_general | solution.py:102
  98.3 12.7 %copy.84 = f32[2,96,128,128]{3,1,0,2:T(8,128)} copy(f32[2,96,128,128]{2,3,0,1:T(8,128)} %fusion.13) | data formatting | bytes 25165824 | tf_op jit(solution)/shard_map/ugpq,grq->ugpr/transpose | solution.py:102
  111.0 9.2 %fusion.19 = f32[32,4,128,128]{3,0,2,1:T(8,128)S(1)} fusion(f32[2,96,128,128]{3,1,0,2:T(8,128)} %copy.84, pred[32,4,96]{2,0,1:T(8,128)(4,1)S(1)} %and_and_fusion, pred[32,2]{0,1:T(4,128)(4,1)S(1)} %compare_and_fusion.1), kind=kOutput, calls=%fused_computation.19 | convolution fusion | flops 4831862784 | bytes 20983872 | tf_op jit(solution)/shard_map/stug,ugpr->stpr/dot_general | solution.py:109
  120.2 22.0 %fusion.16 = f32[32,4,128,128]{2,3,1,0:T(8,128)} fusion(f32[32,4,128,128]{3,0,2,1:T(8,128)S(1)} %fusion.19, f32[32,128,128]{2,1,0:T(8,128)S(1)} %all-to-all-done.1), kind=kOutput, calls=%fused_computation.18 | convolution fusion | flops 3221225472 | bytes 18874368 | tf_op jit(solution)/shard_map/spq,stqr->stpr/dot_general | solution.py:110
  142.3 4.9 %all-to-all-start.2 = ((f32[32,4,128,128]{2,3,1,0:T(8,128)}), f32[32,4,128,128]{2,3,1,0:T(8,128)}, u32[]{:S(2)}, u32[]{:S(2)}) async-start(f32[32,4,128,128]{2,3,1,0:T(8,128)} %fusion.16), calls=%async_computation.2 | async-start | bytes 16777216 | tf_op jit(solution)/shard_map/all_to_all | solution.py:111
  147.1 0.1 reduce_sum.52
  147.2 0.1 mul.76
  147.3 126.6 %all-to-all-done.2 = f32[32,4,128,128]{2,3,1,0:T(8,128)} async-done(((f32[32,4,128,128]{2,3,1,0:T(8,128)}), f32[32,4,128,128]{2,3,1,0:T(8,128)}, u32[]{:S(2)}, u32[]{:S(2)}) %all-to-all-start.2) | async-done | bytes 8388640 | tf_op jit(solution)/shard_map/all_to_all | solution.py:111
  274.0 6.0 %gather_fusion.2 = f32[12,4,128,128]{2,3,1,0:T(8,128)} fusion(f32[32,4,128,128]{2,3,1,0:T(8,128)} %all-to-all-done.2, s32[1024]{0:T(1024)S(1)} %pad_clamp_fusion), kind=kCustom, calls=%fused_computation.2 | custom fusion | bytes 6291504 | tf_op jit(solution)/shard_map/jit(_take)/gather | solution.py:112
  279.9 2.4 select_reduce_fusion
  282.3 1.0 copy.86
  (40 shorter events, 0.3 us)
Async XLA Ops:
  0.0 2.2 copy-start
  4.5 7.1 %copy-start.5 = (s32[2,6]{1,0:T(2,128)S(1)}, s32[2,6]{1,0:T(2,128)}, u32[]{:S(2)}) copy-start(s32[2,6]{1,0:T(2,128)} %param.11) | copy-start | bytes 148
  4.5 7.2 %copy-start.6 = (s32[2,4]{1,0:T(2,128)S(1)}, s32[2,4]{1,0:T(2,128)}, u32[]{:S(2)}) copy-start(s32[2,4]{1,0:T(2,128)} %param.16) | copy-start | bytes 100
  4.5 7.2 %copy-start.7 = (s32[2]{0:T(128)S(1)}, s32[2]{0:T(128)}, u32[]{:S(2)}) copy-start(s32[2]{0:T(128)} %param.17) | copy-start | bytes 28
  4.5 46.6 %copy-start.8 = (s32[2]{0:T(128)S(1)}, s32[2]{0:T(128)}, u32[]{:S(2)}) copy-start(s32[2]{0:T(128)} %param.15) | copy-start | bytes 28
  4.5 46.6 %copy-start.2 = (f32[2,5,128,128]{3,2,1,0:T(8,128)S(1)}, f32[2,5,128,128]{3,2,1,0:T(8,128)}, u32[]{:S(2)}) copy-start(f32[2,5,128,128]{3,2,1,0:T(8,128)} %param.13) | copy-start | bytes 1966084
  4.5 46.6 %copy-start.4 = (s32[2,5]{1,0:T(2,128)S(1)}, s32[2,5]{1,0:T(2,128)}, u32[]{:S(2)}) copy-start(s32[2,5]{1,0:T(2,128)} %param.14) | copy-start | bytes 124
  4.5 37.4 %all-to-all-start.1 = ((f32[32,128,128]{2,1,0:T(8,128)}), f32[32,128,128]{2,1,0:T(8,128)S(1)}, u32[]{:S(2)}, u32[]{:S(2)}) async-start(f32[32,128,128]{2,1,0:T(8,128)} %select_select_fusion), calls=%async_computation.1 | async-start | bytes 4194304 | tf_op jit(solution)/shard_map/all_to_all | solution.py:76
  41.9 37.8 %collective-permute-start.3 = (f32[32,128,128]{2,1,0:T(8,128)S(1)}, f32[32,128,128]{2,1,0:T(8,128)}, u32[]{:S(2)}, u32[]{:S(2)}) collective-permute-start(f32[32,128,128]{2,1,0:T(8,128)S(1)} %all-to-all-done.1), channel_id=1, source_target_pairs={{1,0},{2,1},{3,2},{4,3},{5,4},{6,5},{7,6},{8,7},{9,8},{10,9},{11,1... | collective-permute-start | bytes 6291464 | tf_op jit(solution)/shard_map/ppermute | solution.py:16
  44.1 35.7 %collective-permute-start.2 = (f32[32,128,128]{2,1,0:T(8,128)S(1)}, f32[32,128,128]{2,1,0:T(8,128)}, u32[]{:S(2)}, u32[]{:S(2)}) collective-permute-start(f32[32,128,128]{2,1,0:T(8,128)S(1)} %all-to-all-done.1), channel_id=1, source_target_pairs={{0,1},{1,2},{2,3},{3,4},{4,5},{5,6},{6,7},{7,8},{8,9},{9,10},{10,1... | collective-permute-start | bytes 6291464 | tf_op jit(solution)/shard_map/ppermute | solution.py:13
  47.6 9.9 %all-to-all-start = ((s32[16,2,6]{2,1,0:T(2,128)}), s32[16,2,6]{2,1,0:T(2,128)S(1)}, u32[]{:S(2)}, u32[]{:S(2)}) async-start(s32[16,2,6]{2,1,0:T(2,128)} %bitcast.1), calls=%async_computation | async-start | bytes 32768 | tf_op jit(solution)/shard_map/all_to_all | solution.py:77
  57.5 13.2 %collective-permute-start.1 = (s32[32,6]{1,0:T(8,128)S(1)}, s32[32,6]{1,0:T(8,128)S(1)}, u32[]{:S(2)}, u32[]{:S(2)}) collective-permute-start(s32[32,6]{1,0:T(8,128)S(1)} %bitcast.64), channel_id=1, source_target_pairs={{1,0},{2,1},{3,2},{4,3},{5,4},{6,5},{7,6},{8,7},{9,8},{10,9},{11,1... | collective-permute-start | bytes 2312 | tf_op jit(solution)/shard_map/ppermute | solution.py:16
  57.5 13.2 %collective-permute-start = (s32[32,6]{1,0:T(8,128)S(1)}, s32[32,6]{1,0:T(8,128)S(1)}, u32[]{:S(2)}, u32[]{:S(2)}) collective-permute-start(s32[32,6]{1,0:T(8,128)S(1)} %bitcast.65), channel_id=1, source_target_pairs={{0,1},{1,2},{2,3},{3,4},{4,5},{5,6},{6,7},{7,8},{8,9},{9,10},{10,1... | collective-permute-start | bytes 2312 | tf_op jit(solution)/shard_map/ppermute | solution.py:13
  142.3 5.0 %copy-start.3 = (s32[2,6]{1,0:T(2,128)S(1)}, s32[2,6]{1,0:T(2,128)}, u32[]{:S(2)}) copy-start(s32[2,6]{1,0:T(2,128)} %param.10) | copy-start | bytes 148
  142.3 131.7 %all-to-all-start.2 = ((f32[32,4,128,128]{2,3,1,0:T(8,128)}), f32[32,4,128,128]{2,3,1,0:T(8,128)}, u32[]{:S(2)}, u32[]{:S(2)}) async-start(f32[32,4,128,128]{2,3,1,0:T(8,128)} %fusion.16), calls=%async_computation.2 | async-start | bytes 16777216 | tf_op jit(solution)/shard_map/all_to_all | solution.py:111
  274.0 9.4 %copy-start.1 = (f32[2,6,128,128]{3,2,1,0:T(8,128)S(1)}, f32[2,6,128,128]{3,2,1,0:T(8,128)}, u32[]{:S(2)}) copy-start(f32[2,6,128,128]{3,2,1,0:T(8,128)} %param.9) | copy-start | bytes 2359300
where the time goes:
time: 284 us; the launch traced here: 283 us
  waiting for transfers between devices  171 us (60%)
  matrix products  50.7 us (18%)
  local copies, waits for them, and re-layouts  31.8 us (11%)
  starting transfers between devices  23.1 us (8%)
  other arithmetic  6.07 us (2%)
    all_to_all x1, waiting for transfers between devices, local(): lax.all_to_all(answer, 'row', split_axis=0, concat_axis=0, tiled=True)  127 us
    all_to_all x1, waiting for transfers between devices, local(): lax.all_to_all(outgoing, 'row', split_axis=0, concat_axis=0, tiled=True)  29.7 us
    dot_general x1, matrix products, local(): jnp.einsum('spq,stqr->stpr', arrived, factors, precision=lax.Precision.HI...  22 us
    dot_general x1, matrix products, local(): jnp.einsum('ugpq,grq->ugpr', chosen, ext_blocks, precision=lax.Precision....  18.6 us
    transpose x1, local copies, waits for them, and re-layouts, local(): jnp.einsum('ugpq,grq->ugpr', chosen, ext_blocks, precision=lax.Precision....  12.7 us
    ppermute x2, waiting for transfers between devices, extended(): lax.ppermute(lax.slice_in_dim(block, 0, width, axis=dim), axis, backward)  9.93 us
    dot_general x1, matrix products, local(): jnp.einsum('stug,ugpr->stpr', weight, products, precision=lax.Precision.H...  9.17 us
    gather x1, local copies, waits for them, and re-layouts, local(): chosen = jnp.take(dense_inv, column_index, axis=1)  8.62 us
  transfers between devices with their start and end apart: 7, of which 4 were waited for; matrix products, arithmetic and copies ran while one was open for 4% of the time, Pallas kernels for 0%

commit v1 on v0

v1 whole, which is shorter than its diff:
```python
import functools

import jax
import jax.numpy as jnp
from jax import lax
from jax.experimental import pallas as pl
from jax.experimental.pallas import tpu as pltpu
from jax.sharding import PartitionSpec as P

MESH = pl.DeviceIdType.MESH
F32 = jnp.float32
BF16 = jnp.bfloat16
SIDE = 4


def halves(value):
    high = value.astype(BF16)
    return high, (value - high.astype(F32)).astype(BF16)


def kernel(
    lon_count,
    owner_ref,
    local_ref,
    count_ref,
    cols_ref,
    inv_count_ref,
    pattern_ref,
    pattern_count_ref,
    div_ref,
    inv_ref,
    out_ref,
    inv_all,
    div_all,
    right_parts,
    left_parts,
    factors,
    packet,
    meta,
    places,
    local_sem,
    div_send,
    div_recv,
    meta_send,
    meta_recv,
    inv_send,
    inv_recv,
):
    owners = SIDE * SIDE
    rows, slots_row = owner_ref.shape
    vel_rows, inv_slots = cols_ref.shape
    pattern = pattern_ref.shape[1]
    listed = rows * slots_row
    side = out_ref.shape[2]
    row = lax.axis_index("row")
    col = lax.axis_index("col")
    grid_y, grid_x = row // SIDE, row % SIDE
    nxt = (col + 1) % lon_count
    prv = (col + lon_count - 1) % lon_count

    def at(dy, dx):
        return ((grid_y + dy + SIDE) % SIDE) * SIDE + (grid_x + dx + SIDE) % SIDE

    barrier = pltpu.get_barrier_semaphore()

    def greet(step, carry):
        pl.semaphore_signal(
            barrier, inc=1, device_id=((row + step) % owners, col), device_id_type=MESH
        )
        return carry

    lax.fori_loop(1, owners, greet, 0)
    for other in (nxt, prv):
        pl.semaphore_signal(barrier, inc=1, device_id=(row, other), device_id_type=MESH)

    own_inv = pltpu.make_async_copy(
        inv_ref,
        inv_all.at[pl.ds(row * (vel_rows * inv_slots), vel_rows * inv_slots)],
        local_sem.at[0],
    )
    own_div = pltpu.make_async_copy(div_ref, div_all.at[1], local_sem.at[1])
    own_inv.start()
    own_div.start()

    for slot in range(listed):
        p, k = slot // slots_row, slot % slots_row
        key = jnp.where(k < count_ref[p], owner_ref[p, k] * vel_rows + local_ref[p, k], -1)
        packet[0, slot] = key
    for v in range(vel_rows):
        for column in range(3 * vel_rows):
            found = jnp.int32(-1)
            for m in range(inv_slots):
                found = jnp.where(
                    (cols_ref[v, m] == column) & (m < inv_count_ref[v]), m, found
                )
            packet[0, listed + v * 3 * vel_rows + column] = found
    packet_used = listed + 3 * vel_rows * vel_rows

    pl.semaphore_wait(barrier, owners + 1)

    def meta_copy(step, target, slot):
        return pltpu.make_async_remote_copy(
            src_ref=packet,
            dst_ref=meta.at[pl.ds(slot, 1)],
            send_sem=meta_send.at[step],
            recv_sem=meta_recv.at[step],
            device_id=target,
            device_id_type=MESH,
        )

    def send_meta(step, carry):
        meta_copy(step, ((row + step) % owners, col), row).start()
        return carry

    def piece(owner, v, first, length):
        return inv_all.at[pl.ds((owner * vel_rows + v) * inv_slots + first, length)]

    def link(index, src, dst, dy, dx):
        return pltpu.make_async_remote_copy(
            src_ref=src,
            dst_ref=dst,
            send_sem=inv_send.at[index],
            recv_sem=inv_recv.at[index],
            device_id=(at(dy, dx), col),
            device_id_type=MESH,
        )

    def move(v, along_y, amount):
        return (amount, 0) if along_y else (0, amount)

    def number(v, stage, kind):
        return (v * 5 + stage) * 4 + kind

    lines = (0, -1, 1, 2)

    def line_owner(v, stage, along_y, second):
        if stage == 0:
            dy, dx = move(v, along_y, second)
        else:
            q = lines[stage - 1]
            dy, dx = (second, q) if along_y else (q, second)
        return at(dy, dx)

    def copies(v, stage):
        first_y = v == 1
        along_y = first_y if stage == 0 else not first_y
        longer = (inv_slots + 1) // 2 if (stage + v) % 2 == 0 else inv_slots // 2
        full = (0, inv_slots)
        parts = ((1, 0, full), (-1, 0, full), (1, -1, (0, longer)), (-1, 1, (longer, inv_slots - longer)))
        made = []
        for kind, (step, source, (first, length)) in enumerate(parts):
            dy, dx = move(v, along_y, step)
            here = line_owner(v, stage, along_y, source)
            index = number(v, stage, kind)
            if stage <= 1 and kind < 2:
                outgoing = inv_ref.at[pl.ds(v * inv_slots, inv_slots)]
            else:
                outgoing = piece(here, v, first, length)
            send = link(index, outgoing, piece(here, v, first, length), dy, dx)
            coming = line_owner(v, stage, along_y, source - step)
            arriving = piece(coming, v, first, length)
            recv = link(index, arriving, arriving, dy, dx)
            made.append((send, recv))
        return made

    table = {(v, stage): copies(v, stage) for v in range(vel_rows) for stage in range(5)}

    def start(v, stage, *kinds):
        for kind in kinds:
            table[v, stage][kind][0].start()

    def arrive(v, stage, *kinds):
        for kind in kinds:
            table[v, stage][kind][1].wait_recv()

    both = range(vel_rows)
    for v in both:
        start(v, 0, 0, 1)
    lax.fori_loop(1, owners, send_meta, 0)
    meta_next = meta_copy(0, (row, nxt), owners)
    meta_prev = meta_copy(owners, (row, prv), owners + 1)
    meta_next.start()
    meta_prev.start()
    div_next = pltpu.make_async_remote_copy(
        src_ref=div_ref,
        dst_ref=div_all.at[0],
        send_sem=div_send.at[0],
        recv_sem=div_recv.at[0],
        device_id=(row, nxt),
        device_id_type=MESH,
    )
    div_prev = pltpu.make_async_remote_copy(
        src_ref=div_ref,
        dst_ref=div_all.at[2],
        send_sem=div_send.at[1],
        recv_sem=div_recv.at[1],
        device_id=(row, prv),
        device_id_type=MESH,
    )
    div_next.start()
    div_prev.start()
    for v in both:
        start(v, 1, 0, 1)

    def fill_meta(index, carry):
        meta[row, index] = packet[0, index]
        return carry

    lax.fori_loop(0, packet_used, fill_meta, 0)
    own_inv.wait()
    own_div.wait()

    for v in both:
        arrive(v, 0, 0)
        start(v, 0, 2)
        start(v, 2, 0, 1)
        arrive(v, 0, 1)
        start(v, 0, 3)
        start(v, 3, 0, 1)

    def left_part(p, carry):
        for k in range(slots_row):
            high, low = halves(div_all[1, p * slots_row + k])
            left_parts[p, :, k * side : (k + 1) * side] = high
            left_parts[p, :, (slots_row + k) * side : (slots_row + k + 1) * side] = low
        return carry

    lax.fori_loop(0, rows, left_part, 0)

    def take_meta(step, carry):
        meta_copy(step, ((row + step) % owners, col), (row + owners - step) % owners).wait_recv()
        return carry

    lax.fori_loop(1, owners, take_meta, 0)
    meta_copy(0, (row, nxt), owners).wait_recv()
    meta_copy(owners, (row, prv), owners + 1).wait_recv()
    div_next.wait_recv()
    div_prev.wait_recv()

    for v in both:
        arrive(v, 1, 0)
        start(v, 1, 2)
        arrive(v, 1, 1)
        start(v, 1, 3)

    def right_part(slot, carry):
        p = slot // slots_row
        key = packet[0, slot]
        live = key >= 0
        key = jnp.maximum(key, 0)
        owner, v = key // vel_rows, key % vel_rows
        for t, (shift, device, keys_at) in enumerate(
            ((1, 1, row), (1, 1, row), (2, 2, owners + 1), (0, 0, owners))
        ):
            base = (pattern_ref[p, t] % rows) * slots_row
            for u in range(vel_rows):
                column = shift * vel_rows + u
                place = meta[owner, listed + v * 3 * vel_rows + column]
                wanted = owner * vel_rows + u
                first, second = jnp.int32(-1), jnp.int32(-1)
                for l in range(slots_row):
                    hit = meta[keys_at, base + l] == wanted
                    second = jnp.where(hit, first, second)
                    first = jnp.where(hit, l, first)
                good = live & (t < pattern_count_ref[p]) & (place >= 0)
                one = jnp.where(good & (first >= 0), 1.0, 0.0)
                two = jnp.where(good & (second >= 0), 1.0, 0.0)
                value = (
                    one * div_all[device, base + jnp.maximum(first, 0)]
                    + two * div_all[device, base + jnp.maximum(second, 0)]
                )
                high, low = halves(value)
                lines_at = pl.ds(t * side, side)
                right_parts[slot, lines_at, u * side : (u + 1) * side] = high
                right_parts[slot, lines_at, (vel_rows + u) * side : (vel_rows + u + 1) * side] = low
                if t != 1:
                    places[slot, column] = key * inv_slots + jnp.maximum(place, 0)
        return carry

    lax.fori_loop(0, listed, right_part, 0)

    for v in both:
        arrive(v, 0, 2, 3)
        start(v, 4, 0, 1)
    for stage in (2, 3):
        for v in both:
            arrive(v, stage, 0)
            start(v, stage, 2)
            arrive(v, stage, 1)
            start(v, stage, 3)
    for v in both:
        arrive(v, 4, 0)
        start(v, 4, 2)
        arrive(v, 4, 1)
        start(v, 4, 3)
    for stage in (1, 2, 3, 4):
        for v in both:
            arrive(v, stage, 2, 3)

    width = vel_rows * side

    def answer(p, carry):
        def one_slot(k, inner):
            slot = p * slots_row + k
            for shift, t, wide in ((0, 3, 1), (1, 0, 2), (2, 2, 1)):
                blocks = [
                    halves(inv_all[places[slot, shift * vel_rows + u]]) for u in range(vel_rows)
                ]
                high = jnp.concatenate([b[0] for b in blocks], axis=1)
                low = jnp.concatenate([b[1] for b in blocks], axis=1)
                given = right_parts[slot, t * side : (t + wide) * side, :]
                given_high, given_low = given[:, :width], given[:, width:]
                product = lax.dot_general(
                    jnp.concatenate([high, high, low], axis=1),
                    jnp.concatenate([given_high, given_low, given_high], axis=1),
                    (((1,), (1,)), ((), ())),
                    preferred_element_type=F32,
                )
                product_high, product_low = halves(product)
                here = pl.ds(pl.multiple_of(k * side, side), side)
                factors[0, here, t * side : (t + wide) * side] = product_high
                factors[1, here, t * side : (t + wide) * side] = product_low
            return inner

        lax.fori_loop(0, slots_row, one_slot, 0)
        depth = slots_row * side
        left_high = left_parts[p, :, :depth]
        left_low = left_parts[p, :, depth:]
        result = (
            jnp.dot(left_high, factors[0], preferred_element_type=F32)
            + jnp.dot(left_high, factors[1], preferred_element_type=F32)
            + jnp.dot(left_low, factors[0], preferred_element_type=F32)
        )
        for t in range(pattern):
            out_ref[p, t] = result[:, t * side : (t + 1) * side]
        return carry

    lax.fori_loop(0, rows, answer, 0)

    def sent_meta(step, carry):
        meta_copy(step, ((row + step) % owners, col), row).wait_send()
        return carry

    lax.fori_loop(1, owners, sent_meta, 0)
    meta_next.wait_send()
    meta_prev.wait_send()
    div_next.wait_send()
    div_prev.wait_send()
    for pairs in table.values():
        for send, _ in pairs:
            send.wait_send()


def local(
    lon_count,
    div_blocks,
    div_owner,
    div_local,
    div_count,
    inv_blocks,
    inv_cols,
    inv_count,
    schur_cols,
    schur_count,
):
    rows, slots_row, side, _ = div_blocks.shape
    vel_rows, inv_slots = inv_cols.shape
    pattern = schur_cols.shape[1]
    listed = rows * slots_row
    owners = SIDE * SIDE
    smem = pl.BlockSpec(memory_space=pltpu.SMEM)
    anywhere = pl.BlockSpec(memory_space=pl.ANY)
    return pl.pallas_call(
        functools.partial(kernel, lon_count),
        out_shape=jax.ShapeDtypeStruct((rows, pattern, side, side), F32),
        in_specs=[smem] * 7 + [anywhere] * 2,
        out_specs=pl.BlockSpec(memory_space=pltpu.VMEM),
        scratch_shapes=[
            pltpu.VMEM((owners * vel_rows * inv_slots, side, side), F32),
            pltpu.VMEM((3, listed, side, side), F32),
            pltpu.VMEM((listed, pattern * side, 2 * vel_rows * side), BF16),
            pltpu.VMEM((rows, side, 2 * slots_row * side), BF16),
            pltpu.VMEM((2, slots_row * side, pattern * side), BF16),
            pltpu.SMEM((1, 128), jnp.int32),
            pltpu.SMEM((owners + 2, 128), jnp.int32),
            pltpu.SMEM((listed, 3 * vel_rows), jnp.int32),
            pltpu.SemaphoreType.DMA((2,)),
            pltpu.SemaphoreType.DMA((2,)),
            pltpu.SemaphoreType.DMA((2,)),
            pltpu.SemaphoreType.DMA((owners + 1,)),
            pltpu.SemaphoreType.DMA((owners + 1,)),
            pltpu.SemaphoreType.DMA((40,)),
            pltpu.SemaphoreType.DMA((40,)),
        ],
        compiler_params=pltpu.CompilerParams(
            collective_id=0, has_side_effects=True, vmem_limit_bytes=40 * 2**20
        ),
    )(
        div_owner,
        div_local,
        div_count,
        inv_cols,
        inv_count,
        schur_cols,
        schur_count,
        div_blocks.reshape(listed, side, side),
        inv_blocks.reshape(vel_rows * inv_slots, side, side),
    )


def solution(mesh):
    placed = (
        P(("row", "col"), None, None, None),
        P(("row", "col"), None),
        P(("row", "col"), None),
        P(("row", "col")),
        P(("row", "col"), None, None, None),
        P(("row", "col"), None),
        P(("row", "col")),
        P(("row", "col"), None),
        P(("row", "col")),
    )
    return jax.shard_map(
        functools.partial(local, mesh.shape["col"]),
        mesh=mesh,
        in_specs=placed,
        out_specs=P(("row", "col"), None, None, None),
        check_vma=False,
    )
```

time: 284 us -> 75.1 us (0.26)
  the two profiles are of different devices: /device:TPU:97 before, /device:TPU:2 now
where the time goes in v1:
time: 75.1 us; the launch traced here: 74.8 us
  Pallas kernels  69.1 us (92%)
  local copies, waits for them, and re-layouts  5.7 us (8%)
    pallas_call x1, Pallas kernels, local(): pl.pallas_call(functools.partial(kernel, lon_count), out_shape=jax.ShapeD...  69.1 us
    unnamed x19, local copies, waits for them, and re-layouts  5.7 us

profile of v1, /device:TPU:2, one launch (start us, length us, event | category | flops | bytes accessed | tf_op | source)
XLA Modules:
  0.0 74.8 jit_solution(13235705780826464707)
XLA Ops:
  0.0 0.0 copy-start.3
  0.0 0.0 copy-start.4
  0.0 0.0 copy-start.2
  0.0 0.0 copy-start.6
  0.0 0.7 copy-done.3
  0.7 0.0 copy-done.4
  0.7 0.0 copy-done.2
  0.7 0.0 copy-done.6
  0.7 0.0 copy-start
  0.7 1.1 %copy-done = f32[2,6,128,128]{3,2,1,0:T(8,128)S(1)} copy-done((f32[2,6,128,128]{3,2,1,0:T(8,128)S(1)}, f32[2,6,128,128]{3,2,1,0:T(8,128)}, u32[]{:S(2)}) %copy-start) | copy-done | bytes 786456
  1.8 0.0 copy-start.1
  1.9 1.1 %copy-done.1 = f32[2,5,128,128]{3,2,1,0:T(8,128)S(1)} copy-done((f32[2,5,128,128]{3,2,1,0:T(8,128)S(1)}, f32[2,5,128,128]{3,2,1,0:T(8,128)}, u32[]{:S(2)}) %copy-start.1) | copy-done | bytes 655384
  2.9 0.0 copy-start.5
  2.9 0.7 copy-done.5
  3.6 0.0 copy-start.7
  3.6 0.7 copy-done.7
  4.3 0.0 copy-start.8
  4.3 0.7 copy-done.8
  4.9 69.1 %shard_map.91 = f32[2,4,128,128]{3,2,1,0:T(8,128)S(1)} custom-call(s32[2,6]{1,0:T(2,128)S(1)} %copy-done.2, s32[2,6]{1,0:T(2,128)S(1)} %copy-done.3, s32[2]{0:T(128)S(1)} %copy-done.6, s32[2,5]{1,0:T(2,128)S(1)} %copy-done.4, s32[2]{0:T(128)S(1)} %copy-done.7, s32[2,4]{1,0:T(2,128)S(1)} %copy-done.5, s32[2]{0:T(128)S(1)} %copy-done.8, ...), custom_call_target="tpu_custom_call" | custom-call | tf_op jit(solution)/shard_map/pallas_call | solution.py:373
  74.0 0.8 %copy.11 = f32[2,4,128,128]{3,2,1,0:T(8,128)} copy(f32[2,4,128,128]{3,2,1,0:T(8,128)S(1)} %shard_map.91) | data formatting | bytes 1048576
Async XLA Ops:
  0.0 0.7 copy-start.3
  0.0 0.7 copy-start.4
  0.0 0.7 copy-start.2
  0.0 0.7 copy-start.6
  0.7 1.1 %copy-start = (f32[2,6,128,128]{3,2,1,0:T(8,128)S(1)}, f32[2,6,128,128]{3,2,1,0:T(8,128)}, u32[]{:S(2)}) copy-start(f32[2,6,128,128]{3,2,1,0:T(8,128)} %param.9) | copy-start | bytes 2359300
  1.8 1.1 %copy-start.1 = (f32[2,5,128,128]{3,2,1,0:T(8,128)S(1)}, f32[2,5,128,128]{3,2,1,0:T(8,128)}, u32[]{:S(2)}) copy-start(f32[2,5,128,128]{3,2,1,0:T(8,128)} %param.13) | copy-start | bytes 1966084
  2.9 0.7 copy-start.5
  3.6 0.7 copy-start.7
  4.3 0.7 copy-start.8

commit v2 on v0

v2 whole, which is shorter than its diff:
```python
import functools

import jax
import jax.numpy as jnp
from jax import lax
from jax.experimental import pallas as pl
from jax.experimental.pallas import tpu as pltpu
from jax.sharding import PartitionSpec as P

MESH = pl.DeviceIdType.MESH
F32 = jnp.float32
BF16 = jnp.bfloat16
SIDE = 4
CLASS = 8
META_WIDTH = 128


def halves(value):
    high = value.astype(BF16)
    return high, (value - high.astype(F32)).astype(BF16)


def kernel(
    lon_count,
    owner_hbm,
    local_hbm,
    count_hbm,
    cols_hbm,
    inv_count_hbm,
    pattern_hbm,
    pattern_count_hbm,
    div_ref,
    inv_ref,
    out_ref,
    inv_all,
    div_own,
    div_mate,
    div_pass,
    right_parts,
    left_parts,
    factors,
    mate_sum,
    given_sum,
    packet,
    meta,
    places,
    owner_ref,
    local_ref,
    count_ref,
    cols_ref,
    inv_count_ref,
    pattern_ref,
    pattern_count_ref,
    local_sem,
    div_send,
    div_recv,
    meta_send,
    meta_recv,
    inv_send,
    inv_recv,
    sum_send,
    sum_recv,
):
    rows, slots_row = owner_ref.shape
    vel_rows, inv_slots = cols_ref.shape
    pattern = pattern_ref.shape[1]
    listed = rows * slots_row
    columns = 3 * vel_rows
    side = out_ref.shape[2]
    row = lax.axis_index("row")
    col = lax.axis_index("col")
    odd = col % 2
    nxt = (col + 1) % lon_count
    prv = (col + lon_count - 1) % lon_count
    step_u = 1 + (SIDE - 1) * odd
    step_w = SIDE - (SIDE - 1) * odd
    u = (row // step_u) % SIDE
    w = (row // step_w) % SIDE
    half = u // 2

    def at(u_at, w_at):
        return u_at * step_u + w_at * step_w

    def ring(amount):
        return (w + amount + SIDE) % SIDE

    mate_row = at(u + 1 - 2 * (u % 2), w)
    other_row = at(u, w + 1 - 2 * (w % 2))
    across = at(SIDE - 1 - u, w)

    small = [
        pltpu.make_async_copy(src, dst, local_sem.at[i])
        for i, (src, dst) in enumerate(
            (
                (owner_hbm, owner_ref),
                (local_hbm, local_ref),
                (count_hbm, count_ref),
                (cols_hbm, cols_ref),
                (inv_count_hbm, inv_count_ref),
                (pattern_hbm, pattern_ref),
                (pattern_count_hbm, pattern_count_ref),
            )
        )
    ]
    for copy in small:
        copy.start()
    mine = w * 2 + half
    piece_rows = vel_rows * inv_slots
    own_inv = pltpu.make_async_copy(
        inv_ref, inv_all.at[pl.ds(mine * piece_rows, piece_rows)], local_sem.at[7]
    )
    own_div = pltpu.make_async_copy(div_ref, div_own.at[pl.ds(0, listed)], local_sem.at[8])
    own_inv.start()
    own_div.start()

    kin = [(at(u, ring(k)), col) for k in (1, 2, 3)]
    kin += [(at(SIDE - 1 - u, ring(k)), col) for k in (0, 1, 2, 3)]
    near = [(mate_row, col), (row, nxt), (row, prv), (other_row, nxt), (other_row, prv)]
    heard = [(mate_row, nxt), (mate_row, prv)]
    barrier = pltpu.get_barrier_semaphore()
    for peer in kin + near + heard:
        pl.semaphore_signal(barrier, inc=1, device_id=peer, device_id_type=MESH)

    for copy in small:
        copy.wait()
    inv_at = listed
    pattern_at = inv_at + vel_rows * columns
    used = pattern_at + rows * pattern
    own_key = CLASS

    def note(place, value):
        packet[0, place] = value
        meta[mine, place] = value
        meta[own_key, place] = value

    for slot in range(listed):
        p, k = slot // slots_row, slot % slots_row
        note(slot, jnp.where(k < count_ref[p], owner_ref[p, k] * vel_rows + local_ref[p, k], -1))
    for v in range(vel_rows):
        for column in range(columns):
            found = jnp.int32(-1)
            for m in range(inv_slots):
                hit = (cols_ref[v, m] == column) & (m < inv_count_ref[v])
                found = jnp.where(hit, m, found)
            note(inv_at + v * columns + column, found)
    for p in range(rows):
        for t in range(pattern):
            note(
                pattern_at + p * pattern + t,
                jnp.where(t < pattern_count_ref[p], pattern_ref[p, t] % rows, -1),
            )

    pl.semaphore_wait(barrier, len(kin + near + heard))

    sends = []

    def remote(src, dst, send, recv, target):
        return pltpu.make_async_remote_copy(
            src_ref=src,
            dst_ref=dst,
            send_sem=send,
            recv_sem=recv,
            device_id=target,
            device_id_type=MESH,
        )

    meta_rows = [mine] * 7 + [own_key + 3, own_key + 1, own_key + 2, own_key + 4, own_key + 5]
    from_rows = [ring(-k) * 2 + half for k in (1, 2, 3)]
    from_rows += [ring(-k) * 2 + (1 - half) for k in (0, 1, 2, 3)]
    from_rows += meta_rows[7:]
    meta_in = []
    for i, peer in enumerate(kin + near):
        send = remote(
            packet, meta.at[pl.ds(meta_rows[i], 1)], meta_send.at[i], meta_recv.at[i], peer
        )
        send.start()
        sends.append(send)
        arrived = meta.at[pl.ds(from_rows[i], 1)]
        meta_in.append(remote(packet, arrived, meta_send.at[i], meta_recv.at[i], peer))

    def piece(w_at, b, v, first, length):
        return inv_all.at[pl.ds((w_at * 2 + b) * piece_rows + v * inv_slots + first, length)]

    made = []

    def exchange(outgoing, placed, coming, target):
        index = len(made)
        send = remote(outgoing, placed, inv_send.at[index], inv_recv.at[index], (target, col))
        recv = remote(coming, coming, inv_send.at[index], inv_recv.at[index], (target, col))
        made.append(send)
        return send, recv

    def own_piece(v):
        return inv_ref.at[pl.ds(v * inv_slots, inv_slots)]

    def ring_copies(v, b, source, cut):
        copies = []
        for way in (1, -1):
            copies.append(
                exchange(
                    source,
                    piece(w, b, v, 0, inv_slots),
                    piece(ring(-way), b, v, 0, inv_slots),
                    at(u, ring(way)),
                )
            )
        for way, first, length in ((1, 0, cut), (-1, cut, inv_slots - cut)):
            passed = piece(ring(-way), b, v, first, length)
            copies.append(
                exchange(
                    passed, passed, piece(ring(-2 * way), b, v, first, length), at(u, ring(way))
                )
            )
        return copies

    def cross_copy(v, amount, source, first, length):
        given = piece(ring(amount), half, v, first, length) if source is None else source
        return exchange(
            given,
            piece(ring(amount), half, v, first, length),
            piece(ring(amount), 1 - half, v, first, length),
            across,
        )

    cut = (inv_slots + 1) // 2
    cross_first = cross_copy(0, 0, own_piece(0), 0, inv_slots)
    ring_own = ring_copies(0, half, own_piece(0), cut)
    ring_far = ring_copies(0, 1 - half, piece(w, 1 - half, 0, 0, inv_slots), inv_slots - cut)
    ring_last = ring_copies(1, half, own_piece(1), cut)
    cross_last = [
        cross_copy(1, 0, own_piece(1), 0, inv_slots),
        cross_copy(1, -1, None, 0, inv_slots),
        cross_copy(1, 1, None, 0, inv_slots),
        cross_copy(1, 2, None, 0, cut),
        cross_copy(1, 2, None, cut, inv_slots - cut),
    ]

    def start(pair):
        pair[0].start()

    def arrive(pair):
        pair[1].wait_recv()

    def blocks(buffer, third):
        return buffer.at[pl.ds(third * listed, listed)]

    div_plan = [
        (div_ref, div_pass, (other_row, col)),
        (div_ref, blocks(div_mate, 0), (mate_row, col)),
        (div_ref, blocks(div_own, 1), (row, nxt)),
        (div_ref, blocks(div_own, 2), (row, prv)),
        (div_pass, blocks(div_mate, 1), (row, nxt)),
        (div_pass, blocks(div_mate, 2), (row, prv)),
    ]
    div_copies = [
        remote(src, dst, div_send.at[i], div_recv.at[i], peer)
        for i, (src, dst, peer) in enumerate(div_plan)
    ]

    start(cross_first)
    start(ring_last[0])
    start(ring_last[1])
    for copy in div_copies[:4]:
        copy.start()
    start(ring_own[0])
    start(ring_own[1])
    start(cross_last[0])
    own_inv.wait()
    own_div.wait()

    arrive(cross_first)
    start(ring_far[0])
    start(ring_far[1])
    arrive(ring_last[0])
    start(ring_last[2])
    start(cross_last[1])
    arrive(ring_last[1])
    start(ring_last[3])
    start(cross_last[2])

    def left_part(group, source):
        def one(p, carry):
            for k in range(slots_row):
                high, low = halves(source[p * slots_row + k])
                left_parts[group, p, :, k * side : (k + 1) * side] = high
                left_parts[group, p, :, (slots_row + k) * side : (slots_row + k + 1) * side] = low
            return carry

        lax.fori_loop(0, rows, one, 0)

    left_part(0, div_own)
    for copy in meta_in:
        copy.wait_recv()

    arrive(ring_own[0])
    start(ring_own[2])
    arrive(ring_own[1])
    start(ring_own[3])
    div_copies[0].wait_recv()
    div_copies[4].start()
    div_copies[5].start()
    div_copies[2].wait_recv()
    div_copies[3].wait_recv()

    def right_part(group, source):
        keys_own = own_key + 3 * group

        def one(slot, carry):
            p = slot // slots_row
            key = meta[keys_own, slot]
            live = key >= 0
            key = jnp.maximum(key, 0)
            owner, v = key // vel_rows, key % vel_rows
            owner_y, owner_x = owner // SIDE, owner % SIDE
            owner_u = owner_x + odd * (owner_y - owner_x)
            owner_w = owner_y + odd * (owner_x - owner_y)
            live = live & (((owner_u + 1) // 2) % 2 == ((u + 1) // 2) % 2)
            found = owner_w * 2 + owner_u // 2
            for t, (shift, third) in enumerate(((1, 0), (1, 0), (2, 2), (0, 1))):
                wanted_row = meta[keys_own, pattern_at + p * pattern + t]
                chosen = live & (wanted_row >= 0)
                base = jnp.maximum(wanted_row, 0) * slots_row
                for c in range(vel_rows):
                    column = shift * vel_rows + c
                    place = meta[found, inv_at + v * columns + column]
                    wanted = owner * vel_rows + c
                    first, second = jnp.int32(-1), jnp.int32(-1)
                    for l in range(slots_row):
                        hit = meta[keys_own + third, base + l] == wanted
                        second = jnp.where(hit, first, second)
                        first = jnp.where(hit, l, first)
                    good = chosen & (place >= 0)
                    one_on = jnp.where(good & (first >= 0), 1.0, 0.0)
                    two_on = jnp.where(good & (second >= 0), 1.0, 0.0)
                    here = third * listed + base
                    value = (
                        one_on * source[here + jnp.maximum(first, 0)]
                        + two_on * source[here + jnp.maximum(second, 0)]
                    )
                    high, low = halves(value)
                    lines = pl.ds(t * side, side)
                    at_slot = group * listed + slot
                    right_parts[at_slot, lines, c * side : (c + 1) * side] = high
                    right_parts[
                        at_slot, lines, (vel_rows + c) * side : (vel_rows + c + 1) * side
                    ] = low
                    if t != 1:
                        places[at_slot, column] = (
                            found * piece_rows + v * inv_slots + jnp.maximum(place, 0)
                        )
            return carry

        lax.fori_loop(0, listed, one, 0)

    right_part(0, div_own)

    arrive(ring_last[2])
    start(cross_last[3])
    arrive(ring_last[3])
    start(cross_last[4])
    arrive(ring_far[0])
    start(ring_far[2])
    arrive(ring_far[1])
    start(ring_far[3])

    div_copies[1].wait_recv()
    div_copies[4].wait_recv()
    div_copies[5].wait_recv()
    left_part(1, div_mate)
    right_part(1, div_mate)

    for pair in (*ring_own[2:], *cross_last, *ring_far[2:]):
        arrive(pair)

    width = vel_rows * side

    def answer(group, p, target):
        def one_slot(k, carry):
            slot = group * listed + p * slots_row + k
            for shift, t, wide in ((0, 3, 1), (1, 0, 2), (2, 2, 1)):
                parts = [halves(inv_all[places[slot, shift * vel_rows + c]]) for c in range(vel_rows)]
                high = jnp.concatenate([part[0] for part in parts], axis=1)
                low = jnp.concatenate([part[1] for part in parts], axis=1)
                given = right_parts[slot, t * side : (t + wide) * side, :]
                given_high, given_low = given[:, :width], given[:, width:]
                product = lax.dot_general(
                    jnp.concatenate([high, high, low], axis=1),
                    jnp.concatenate([given_high, given_low, given_high], axis=1),
                    (((1,), (1,)), ((), ())),
                    preferred_element_type=F32,
                )
                product_high, product_low = halves(product)
                here = pl.ds(pl.multiple_of(k * side, side), side)
                factors[0, here, t * side : (t + wide) * side] = product_high
                factors[1, here, t * side : (t + wide) * side] = product_low
            return carry

        lax.fori_loop(0, slots_row, one_slot, 0)
        depth = slots_row * side
        left_high = left_parts[group, p, :, :depth]
        left_low = left_parts[group, p, :, depth:]
        result = (
            jnp.dot(left_high, factors[0], preferred_element_type=F32)
            + jnp.dot(left_high, factors[1], preferred_element_type=F32)
            + jnp.dot(left_low, factors[0], preferred_element_type=F32)
        )
        for t in range(pattern):
            target[p, t] = result[:, t * side : (t + 1) * side]

    returns = [
        remote(
            mate_sum.at[pl.ds(p, 1)],
            given_sum.at[pl.ds(p, 1)],
            sum_send.at[p],
            sum_recv.at[p],
            (mate_row, col),
        )
        for p in range(rows)
    ]
    for p in range(rows):
        answer(1, p, mate_sum)
        returns[p].start()
    for p in range(rows):
        answer(0, p, out_ref)
    for p in range(rows):
        returns[p].wait_recv()
        out_ref[p] = out_ref[p] + given_sum[p]

    for copy in (*sends, *div_copies, *made, *returns):
        copy.wait_send()


def local(
    lon_count,
    div_blocks,
    div_owner,
    div_local,
    div_count,
    inv_blocks,
    inv_cols,
    inv_count,
    schur_cols,
    schur_count,
):
    rows, slots_row, side, _ = div_blocks.shape
    vel_rows, inv_slots = inv_cols.shape
    pattern = schur_cols.shape[1]
    listed = rows * slots_row
    width = pattern * side
    ints = (div_owner, div_local, div_count, inv_cols, inv_count, schur_cols, schur_count)
    operands = [
        pltpu.with_memory_space_constraint(value, pltpu.HBM)
        for value in (
            *ints,
            div_blocks.reshape(listed, side, side),
            inv_blocks.reshape(vel_rows * inv_slots, side, side),
        )
    ]
    return pl.pallas_call(
        functools.partial(kernel, lon_count),
        out_shape=jax.ShapeDtypeStruct((rows, pattern, side, side), F32),
        in_specs=[pl.BlockSpec(memory_space=pltpu.HBM)] * len(operands),
        out_specs=pl.BlockSpec(memory_space=pltpu.VMEM),
        scratch_shapes=[
            pltpu.VMEM((CLASS * vel_rows * inv_slots, side, side), F32),
            pltpu.VMEM((3 * listed, side, side), F32),
            pltpu.VMEM((3 * listed, side, side), F32),
            pltpu.VMEM((listed, side, side), F32),
            pltpu.VMEM((2 * listed, width, 2 * vel_rows * side), BF16),
            pltpu.VMEM((2, rows, side, 2 * slots_row * side), BF16),
            pltpu.VMEM((2, slots_row * side, width), BF16),
            pltpu.VMEM((rows, pattern, side, side), F32),
            pltpu.VMEM((rows, pattern, side, side), F32),
            pltpu.SMEM((1, META_WIDTH), jnp.int32),
            pltpu.SMEM((CLASS + 6, META_WIDTH), jnp.int32),
            pltpu.SMEM((2 * listed, 3 * vel_rows), jnp.int32),
            *[pltpu.SMEM(value.shape, jnp.int32) for value in ints],
            pltpu.SemaphoreType.DMA((9,)),
            pltpu.SemaphoreType.DMA((6,)),
            pltpu.SemaphoreType.DMA((6,)),
            pltpu.SemaphoreType.DMA((12,)),
            pltpu.SemaphoreType.DMA((12,)),
            pltpu.SemaphoreType.DMA((18,)),
            pltpu.SemaphoreType.DMA((18,)),
            pltpu.SemaphoreType.DMA((rows,)),
            pltpu.SemaphoreType.DMA((rows,)),
        ],
        compiler_params=pltpu.CompilerParams(
            collective_id=0, has_side_effects=True, vmem_limit_bytes=56 * 2**20
        ),
    )(*operands)


def solution(mesh):
    placed = (
        P(("row", "col"), None, None, None),
        P(("row", "col"), None),
        P(("row", "col"), None),
        P(("row", "col")),
        P(("row", "col"), None, None, None),
        P(("row", "col"), None),
        P(("row", "col")),
        P(("row", "col"), None),
        P(("row", "col")),
    )
    return jax.shard_map(
        functools.partial(local, mesh.shape["col"]),
        mesh=mesh,
        in_specs=placed,
        out_specs=P(("row", "col"), None, None, None),
        check_vma=False,
    )
```

time: 284 us -> 67.8 us (0.24)
  the two profiles are of different devices: /device:TPU:97 before, /device:TPU:2 now
where the time goes in v2:
time: 67.8 us; the launch traced here: 67.6 us
  Pallas kernels  65.7 us (97%)
  local copies, waits for them, and re-layouts  1.87 us (3%)
    pallas_call x1, Pallas kernels, local(): pl.pallas_call(functools.partial(kernel, lon_count), out_shape=jax.ShapeD...  65.7 us
    unnamed x1, local copies, waits for them, and re-layouts  1.87 us

profile of v2, /device:TPU:2, one launch (start us, length us, event | category | flops | bytes accessed | tf_op | source)
XLA Modules:
  0.0 67.6 jit_solution(10652735876118070060)
XLA Ops:
  0.0 65.7 %shard_map.91 = f32[2,4,128,128]{3,2,1,0:T(8,128)} custom-call(s32[2,6]{1,0:T(2,128)} %owner_hbm.1, s32[2,6]{1,0:T(2,128)} %local_hbm.1, s32[2]{0:T(128)} %count_hbm.1, s32[2,5]{1,0:T(2,128)} %cols_hbm.1, s32[2]{0:T(128)} %inv_count_hbm.1, s32[2,4]{1,0:T(2,128)} %pattern_hbm.1, s32[2]{0:T(128)} %pattern_count_hbm.1, f32[12,128,128]{2,1,0:T(8,128)} %bitcast.2, ...), custom_call_target="tpu_custom_call" | custom-call | tf_op jit(solution)/shard_map/pallas_call | solution.py:459
  65.7 1.9 %copy.11 = f32[2,4,128,128]{3,2,1,0:T(8,128)} copy(f32[2,4,128,128]{3,2,1,0:T(8,128)} %shard_map.91) | data formatting | bytes 1048576

commit v3 on v2

v3 whole, which is shorter than its diff:
```python
import functools

import jax
import jax.numpy as jnp
from jax import lax
from jax.experimental import pallas as pl
from jax.experimental.pallas import tpu as pltpu
from jax.sharding import PartitionSpec as P

MESH = pl.DeviceIdType.MESH
F32 = jnp.float32
BF16 = jnp.bfloat16
SIDE = 4
CLASS = 8
META_WIDTH = 128


def halves(value):
    high = value.astype(BF16)
    return high, (value - high.astype(F32)).astype(BF16)


def kernel(
    lon_count,
    owner_hbm,
    local_hbm,
    count_hbm,
    cols_hbm,
    inv_count_hbm,
    pattern_hbm,
    pattern_count_hbm,
    div_ref,
    inv_ref,
    out_ref,
    *scratch,
):
    held = scratch[:CLASS]
    (
        div_own,
        div_own_side,
        div_mate,
        div_mate_side,
        div_pass,
        dense_div,
        dense_inv,
        sums,
        given,
        packet,
        meta,
        owner_ref,
        local_ref,
        count_ref,
        cols_ref,
        inv_count_ref,
        pattern_ref,
        pattern_count_ref,
        local_sem,
        div_send,
        div_recv,
        meta_send,
        meta_recv,
        inv_send,
        inv_recv,
        sum_send,
        sum_recv,
    ) = scratch[CLASS:]
    rows, slots_row = owner_ref.shape
    vel_rows, inv_slots = cols_ref.shape
    pattern = pattern_ref.shape[1]
    listed = rows * slots_row
    columns = 3 * vel_rows
    side = out_ref.shape[2]
    width = vel_rows * side
    row = lax.axis_index("row")
    col = lax.axis_index("col")
    odd = col % 2
    nxt = (col + 1) % lon_count
    prv = (col + lon_count - 1) % lon_count
    step_u = 1 + (SIDE - 1) * odd
    step_w = SIDE - (SIDE - 1) * odd
    u = (row // step_u) % SIDE
    w = (row // step_w) % SIDE

    def at(u_at, w_at):
        return u_at * step_u + w_at * step_w

    def ring(amount):
        return (w + amount + SIDE) % SIDE

    mate_row = at(u + 1 - 2 * (u % 2), w)
    other_row = at(u, w + 1 - 2 * (w % 2))
    across = at(SIDE - 1 - u, w)

    small = [
        pltpu.make_async_copy(src, dst, local_sem.at[i])
        for i, (src, dst) in enumerate(
            (
                (owner_hbm, owner_ref),
                (local_hbm, local_ref),
                (count_hbm, count_ref),
                (cols_hbm, cols_ref),
                (inv_count_hbm, inv_count_ref),
                (pattern_hbm, pattern_ref),
                (pattern_count_hbm, pattern_count_ref),
            )
        )
    ]
    for copy in small:
        copy.start()
    own_inv = pltpu.make_async_copy(inv_ref, held[0], local_sem.at[7])
    own_div = pltpu.make_async_copy(div_ref, div_own, local_sem.at[8])
    own_inv.start()
    own_div.start()

    kin = [(at(u, ring(k)), col) for k in (1, 2, 3)]
    kin += [(at(SIDE - 1 - u, ring(k)), col) for k in (0, 1, 2, 3)]
    near = [(mate_row, col), (row, nxt), (row, prv), (other_row, nxt), (other_row, prv)]
    heard = [(mate_row, nxt), (mate_row, prv)]
    barrier = pltpu.get_barrier_semaphore()
    for peer in kin + near + heard:
        pl.semaphore_signal(barrier, inc=1, device_id=peer, device_id_type=MESH)

    for copy in small:
        copy.wait()
    inv_at = listed
    pattern_at = inv_at + vel_rows * columns
    own_key = CLASS

    def note(place, value):
        packet[0, place] = value
        meta[0, place] = value
        meta[own_key, place] = value

    for slot in range(listed):
        p, k = slot // slots_row, slot % slots_row
        note(slot, jnp.where(k < count_ref[p], owner_ref[p, k] * vel_rows + local_ref[p, k], -1))
    for v in range(vel_rows):
        for column in range(columns):
            found = jnp.int32(-1)
            for m in range(inv_slots):
                hit = (cols_ref[v, m] == column) & (m < inv_count_ref[v])
                found = jnp.where(hit, m, found)
            note(inv_at + v * columns + column, found)
    for p in range(rows):
        for t in range(pattern):
            note(pattern_at + p * pattern + t, pattern_ref[p, t] % rows)

    pl.semaphore_wait(barrier, len(kin + near + heard))

    def remote(src, dst, send, recv, target):
        return pltpu.make_async_remote_copy(
            src_ref=src,
            dst_ref=dst,
            send_sem=send,
            recv_sem=recv,
            device_id=target,
            device_id_type=MESH,
        )

    def piece(offset, b, v, first, length):
        return held[(offset % SIDE) * 2 + b].at[pl.ds(v * inv_slots + first, length)]

    made = []

    def exchange(outgoing, placed, target):
        index = len(made)
        copy = remote(outgoing, placed, inv_send.at[index], inv_recv.at[index], (target, col))
        made.append(copy)
        return copy

    def own_piece(v):
        return inv_ref.at[pl.ds(v * inv_slots, inv_slots)]

    def ring_copies(v, b, source, cut):
        copies = []
        for way in (1, -1):
            copies.append(
                exchange(source, piece(-way, b, v, 0, inv_slots), at(u, ring(way)))
            )
        for way, first, length in ((1, 0, cut), (-1, cut, inv_slots - cut)):
            copies.append(
                exchange(
                    piece(-way, b, v, first, length),
                    piece(2, b, v, first, length),
                    at(u, ring(way)),
                )
            )
        return copies

    def cross_copy(v, offset, first, length):
        outgoing = own_piece(v) if offset == 0 else piece(offset, 0, v, first, length)
        return exchange(outgoing, piece(offset, 1, v, first, length), across)

    cut = (inv_slots + 1) // 2
    cross_first = cross_copy(0, 0, 0, inv_slots)
    ring_own = ring_copies(0, 0, own_piece(0), cut)
    ring_far = ring_copies(0, 1, piece(0, 1, 0, 0, inv_slots), inv_slots - cut)
    ring_last = ring_copies(1, 0, own_piece(1), cut)
    cross_last = [
        cross_copy(1, 0, 0, inv_slots),
        cross_copy(1, -1, 0, inv_slots),
        cross_copy(1, 1, 0, inv_slots),
        cross_copy(1, 2, 0, cut),
        cross_copy(1, 2, cut, inv_slots - cut),
    ]

    plan = []
    for part in range(2):
        some = pl.ds(part * slots_row, slots_row)
        plan.append((div_ref.at[some], div_pass.at[some], (other_row, col)))
    plan += [
        (div_ref, div_own_side.at[pl.ds(0, listed)], (row, nxt)),
        (div_ref, div_own_side.at[pl.ds(listed, listed)], (row, prv)),
        (div_ref, div_mate, (mate_row, col)),
    ]
    for part in range(2):
        some = pl.ds(part * slots_row, slots_row)
        for third, target in ((1, nxt), (2, prv)):
            there = pl.ds((third - 1) * listed + part * slots_row, slots_row)
            plan.append((div_pass.at[some], div_mate_side.at[there], (row, target)))
    div_copies = [
        remote(src, dst, div_send.at[i], div_recv.at[i], peer)
        for i, (src, dst, peer) in enumerate(plan)
    ]

    meta_rows = [((-k) % SIDE) * 2 for k in (1, 2, 3)]
    meta_rows += [((-k) % SIDE) * 2 + 1 for k in (0, 1, 2, 3)]
    meta_rows += [own_key + 3, own_key + 1, own_key + 2, own_key + 4, own_key + 5]
    meta_copies = [
        remote(packet, meta.at[pl.ds(meta_rows[i], 1)], meta_send.at[i], meta_recv.at[i], peer)
        for i, peer in enumerate(kin + near)
    ]

    div_copies[0].start()
    div_copies[1].start()
    cross_first.start()
    ring_last[0].start()
    ring_last[1].start()
    for copy in meta_copies:
        copy.start()
    div_copies[2].start()
    div_copies[3].start()
    ring_own[0].start()
    ring_own[1].start()
    cross_last[0].start()
    sums[...] = jnp.zeros_like(sums)
    own_inv.wait()
    own_div.wait()

    def spread(group, thirds):
        keys_own = own_key + 3 * group
        home, beside = ((div_own, div_own_side), (div_mate, div_mate_side))[group]

        def one(rel, carry):
            owner_u = u + (rel % 2) * (SIDE - 1 - 2 * u)
            owner = at(owner_u, (w + rel // 2) % SIDE)
            for third in thirds:
                for p in range(rows):
                    base = p * slots_row
                    if third:
                        t = 3 if third == 1 else 2
                        base = meta[keys_own, pattern_at + p * pattern + t] * slots_row
                    for c in range(vel_rows):
                        wanted = owner * vel_rows + c
                        first, second = jnp.int32(-1), jnp.int32(-1)
                        for l in range(slots_row):
                            hit = meta[keys_own + third, base + l] == wanted
                            second = jnp.where(hit, first, second)
                            first = jnp.where(hit, l, first)
                        one_on = jnp.where(first >= 0, 1.0, 0.0)
                        two_on = jnp.where(second >= 0, 1.0, 0.0)
                        source = beside if third else home
                        here = max(third - 1, 0) * listed + base
                        value = (
                            one_on * source[here + jnp.maximum(first, 0)]
                            + two_on * source[here + jnp.maximum(second, 0)]
                        )
                        high, low = halves(value)
                        place = group * CLASS + rel
                        lines = slice(p * side, (p + 1) * side)
                        at_high = slice(c * side, (c + 1) * side)
                        at_low = slice(width + c * side, width + (c + 1) * side)
                        dense_div[place, third, lines, at_high] = high
                        dense_div[place, third, lines, at_low] = low
            return carry

        lax.fori_loop(0, CLASS, one, 0)

    def gather(rel):
        for v in range(vel_rows):
            for column in range(columns):
                place = meta[rel, inv_at + v * columns + column]
                on = jnp.where(place >= 0, 1.0, 0.0)
                high, low = halves(on * held[rel][v * inv_slots + jnp.maximum(place, 0)])
                third = (1, 0, 2)[column // vel_rows]
                c = column % vel_rows
                lines = slice(v * side, (v + 1) * side)
                dense_inv[rel, third, lines, c * side : (c + 1) * side] = high
                dense_inv[rel, third, lines, width + c * side : width + (c + 1) * side] = low

    def product(rel, group, only=None):
        place = group * CLASS + rel
        factors = []
        for third in range(3):
            inv = dense_inv[rel, third]
            div = dense_div[place, third]
            inv_high, inv_low = inv[:, :width], inv[:, width:]
            div_high, div_low = div[:, :width], div[:, width:]
            value = lax.dot_general(
                jnp.concatenate([inv_high, inv_high, inv_low], axis=1),
                jnp.concatenate([div_high, div_low, div_high], axis=1),
                (((1,), (1,)), ((), ())),
                preferred_element_type=F32,
            )
            factors.append(halves(value))
        for p in range(rows):
            order = ((0, p), (0, 1 - p), (2, p), (1, p))
            high, low = (
                jnp.concatenate(
                    [factors[third][i][:, q * side : (q + 1) * side] for third, q in order], axis=1
                )
                for i in range(2)
            )
            left = dense_div[place, 0, p * side : (p + 1) * side, :]
            left_high, left_low = left[:, :width], left[:, width:]
            sums[group, p] += jnp.dot(
                jnp.concatenate([left_high, left_high, left_low], axis=1),
                jnp.concatenate([high, low, high], axis=0),
                preferred_element_type=F32,
            )
            if only is not None:
                only[p].start()

    cross_first.wait_recv()
    ring_far[0].start()
    ring_far[1].start()
    ring_last[0].wait_recv()
    ring_last[2].start()
    cross_last[1].start()
    ring_last[1].wait_recv()
    ring_last[3].start()
    cross_last[2].start()

    spread(0, (0,))

    for part in range(2):
        div_copies[part].wait_recv()
        div_copies[5 + 2 * part].start()
        div_copies[6 + 2 * part].start()
    div_copies[4].start()
    ring_own[0].wait_recv()
    ring_own[2].start()
    ring_own[1].wait_recv()
    ring_own[3].start()
    for copy in meta_copies:
        copy.wait_recv()
    div_copies[2].wait_recv()
    div_copies[3].wait_recv()
    spread(0, (1, 2))
    ring_last[2].wait_recv()
    cross_last[3].start()
    ring_last[3].wait_recv()
    cross_last[4].start()
    gather(0)
    product(0, 0)
    ring_far[0].wait_recv()
    ring_far[2].start()
    ring_far[1].wait_recv()
    ring_far[3].start()
    cross_last[0].wait_recv()
    early = (1, 6, 2)
    for rel in early:
        gather(rel)
        product(rel, 0)
    for copy in div_copies[4:]:
        copy.wait_recv()
    spread(1, (0, 1, 2))
    for rel in (0, *early):
        product(rel, 1)
    ring_own[2].wait_recv()
    ring_own[3].wait_recv()
    gather(4)
    product(4, 0)
    product(4, 1)
    for rel, copy in ((7, cross_last[1]), (3, cross_last[2])):
        copy.wait_recv()
        gather(rel)
        product(rel, 0)
        product(rel, 1)
    for copy in (*cross_last[3:], *ring_far[2:]):
        copy.wait_recv()
    gather(5)
    returns = [
        remote(
            sums.at[1, pl.ds(p, 1)],
            given.at[pl.ds(p, 1)],
            sum_send.at[p],
            sum_recv.at[p],
            (mate_row, col),
        )
        for p in range(rows)
    ]
    product(5, 1, returns)
    product(5, 0)
    for p in range(rows):
        returns[p].wait_recv()
        total = sums[0, p] + given[p]
        for t in range(pattern):
            kept = jnp.where(t < pattern_count_ref[p], 1.0, 0.0)
            out_ref[p, t] = kept * total[:, t * side : (t + 1) * side]

    for copy in (*meta_copies, *div_copies, *made, *returns):
        copy.wait_send()


def local(
    lon_count,
    div_blocks,
    div_owner,
    div_local,
    div_count,
    inv_blocks,
    inv_cols,
    inv_count,
    schur_cols,
    schur_count,
):
    rows, slots_row, side, _ = div_blocks.shape
    vel_rows, inv_slots = inv_cols.shape
    pattern = schur_cols.shape[1]
    listed = rows * slots_row
    width = pattern * side
    ints = (div_owner, div_local, div_count, inv_cols, inv_count, schur_cols, schur_count)
    operands = [
        pltpu.with_memory_space_constraint(value, pltpu.HBM)
        for value in (
            *ints,
            div_blocks.reshape(listed, side, side),
            inv_blocks.reshape(vel_rows * inv_slots, side, side),
        )
    ]
    return pl.pallas_call(
        functools.partial(kernel, lon_count),
        out_shape=jax.ShapeDtypeStruct((rows, pattern, side, side), F32),
        in_specs=[pl.BlockSpec(memory_space=pltpu.HBM)] * len(operands),
        out_specs=pl.BlockSpec(memory_space=pltpu.VMEM),
        scratch_shapes=[
            *[pltpu.VMEM((vel_rows * inv_slots, side, side), F32)] * CLASS,
            pltpu.VMEM((listed, side, side), F32),
            pltpu.VMEM((2 * listed, side, side), F32),
            pltpu.VMEM((listed, side, side), F32),
            pltpu.VMEM((2 * listed, side, side), F32),
            pltpu.VMEM((listed, side, side), F32),
            pltpu.VMEM((2 * CLASS, 3, rows * side, 2 * vel_rows * side), BF16),
            pltpu.VMEM((CLASS, 3, vel_rows * side, 2 * vel_rows * side), BF16),
            pltpu.VMEM((2, rows, side, width), F32),
            pltpu.VMEM((rows, side, width), F32),
            pltpu.SMEM((1, META_WIDTH), jnp.int32),
            pltpu.SMEM((CLASS + 6, META_WIDTH), jnp.int32),
            *[pltpu.SMEM(value.shape, jnp.int32) for value in ints],
            pltpu.SemaphoreType.DMA((9,)),
            pltpu.SemaphoreType.DMA((9,)),
            pltpu.SemaphoreType.DMA((9,)),
            pltpu.SemaphoreType.DMA((12,)),
            pltpu.SemaphoreType.DMA((12,)),
            pltpu.SemaphoreType.DMA((18,)),
            pltpu.SemaphoreType.DMA((18,)),
            pltpu.SemaphoreType.DMA((rows,)),
            pltpu.SemaphoreType.DMA((rows,)),
        ],
        compiler_params=pltpu.CompilerParams(
            collective_id=0, has_side_effects=True, vmem_limit_bytes=56 * 2**20
        ),
    )(*operands)


def solution(mesh):
    placed = (
        P(("row", "col"), None, None, None),
        P(("row", "col"), None),
        P(("row", "col"), None),
        P(("row", "col")),
        P(("row", "col"), None, None, None),
        P(("row", "col"), None),
        P(("row", "col")),
        P(("row", "col"), None),
        P(("row", "col")),
    )
    return jax.shard_map(
        functools.partial(local, mesh.shape["col"]),
        mesh=mesh,
        in_specs=placed,
        out_specs=P(("row", "col"), None, None, None),
        check_vma=False,
    )
```

time: 67.8 us -> 67.4 us (level)
  the two profiles are of different devices: /device:TPU:2 before, /device:TPU:24 now
where the time goes in v3:
time: 67.4 us; the launch traced here: 67.2 us
  Pallas kernels  65.3 us (97%)
  local copies, waits for them, and re-layouts  1.87 us (3%)
    pallas_call x1, Pallas kernels, local(): pl.pallas_call(functools.partial(kernel, lon_count), out_shape=jax.ShapeD...  65.3 us
    unnamed x1, local copies, waits for them, and re-layouts  1.87 us

profile of v3, /device:TPU:24, one launch (start us, length us, event | category | flops | bytes accessed | tf_op | source)
XLA Modules:
  0.0 67.2 jit_solution(17076488402312823164)
XLA Ops:
  0.0 65.3 %shard_map.91 = f32[2,4,128,128]{3,2,1,0:T(8,128)} custom-call(s32[2,6]{1,0:T(2,128)} %owner_hbm.1, s32[2,6]{1,0:T(2,128)} %local_hbm.1, s32[2]{0:T(128)} %count_hbm.1, s32[2,5]{1,0:T(2,128)} %cols_hbm.1, s32[2]{0:T(128)} %inv_count_hbm.1, s32[2,4]{1,0:T(2,128)} %pattern_hbm.1, s32[2]{0:T(128)} %pattern_count_hbm.1, f32[12,128,128]{2,1,0:T(8,128)} %bitcast.2, ...), custom_call_target="tpu_custom_call" | custom-call | tf_op jit(solution)/shard_map/pallas_call | solution.py:442
  65.3 1.9 %copy.11 = f32[2,4,128,128]{3,2,1,0:T(8,128)} copy(f32[2,4,128,128]{3,2,1,0:T(8,128)} %shard_map.91) | data formatting | bytes 1048576

commit v4 on v3

--- a/solution.py
+++ b/solution.py
@@ -84,8 +84,10 @@
     def at(u_at, w_at):
         return u_at * step_u + w_at * step_w
 
+    turn = 1 - 2 * (w % 2)
+
     def ring(amount):
-        return (w + amount + SIDE) % SIDE
+        return (w + turn * amount + 2 * SIDE) % SIDE
 
     mate_row = at(u + 1 - 2 * (u % 2), w)
     other_row = at(u, w + 1 - 2 * (w % 2))
@@ -175,7 +177,7 @@
         copies = []
         for way in (1, -1):
             copies.append(
-                exchange(source, piece(-way, b, v, 0, inv_slots), at(u, ring(way)))
+                exchange(source, piece(way, b, v, 0, inv_slots), at(u, ring(way)))
             )
         for way, first, length in ((1, 0, cut), (-1, cut, inv_slots - cut)):
             copies.append(
@@ -223,37 +225,21 @@
         for i, (src, dst, peer) in enumerate(plan)
     ]
 
-    meta_rows = [((-k) % SIDE) * 2 for k in (1, 2, 3)]
-    meta_rows += [((-k) % SIDE) * 2 + 1 for k in (0, 1, 2, 3)]
+    meta_rows = [k * 2 for k in (1, 2, 3)]
+    meta_rows += [k * 2 + 1 for k in (0, 1, 2, 3)]
     meta_rows += [own_key + 3, own_key + 1, own_key + 2, own_key + 4, own_key + 5]
     meta_copies = [
         remote(packet, meta.at[pl.ds(meta_rows[i], 1)], meta_send.at[i], meta_recv.at[i], peer)
         for i, peer in enumerate(kin + near)
     ]
 
-    div_copies[0].start()
-    div_copies[1].start()
-    cross_first.start()
-    ring_last[0].start()
-    ring_last[1].start()
-    for copy in meta_copies:
-        copy.start()
-    div_copies[2].start()
-    div_copies[3].start()
-    ring_own[0].start()
-    ring_own[1].start()
-    cross_last[0].start()
-    sums[...] = jnp.zeros_like(sums)
-    own_inv.wait()
-    own_div.wait()
-
     def spread(group, thirds):
         keys_own = own_key + 3 * group
         home, beside = ((div_own, div_own_side), (div_mate, div_mate_side))[group]
 
         def one(rel, carry):
             owner_u = u + (rel % 2) * (SIDE - 1 - 2 * u)
-            owner = at(owner_u, (w + rel // 2) % SIDE)
+            owner = at(owner_u, ring(rel // 2))
             for third in thirds:
                 for p in range(rows):
                     base = p * slots_row
@@ -331,64 +317,92 @@
             if only is not None:
                 only[p].start()
 
+    cross_first.start()
+    ring_last[0].start()
+    ring_last[1].start()
+    ring_own[0].start()
+    ring_own[1].start()
+    cross_last[0].start()
+    div_copies[4].start()
+    div_copies[2].start()
+    div_copies[3].start()
+    div_copies[0].start()
+    div_copies[1].start()
+    for copy in meta_copies:
+        copy.start()
+    sums[...] = jnp.zeros_like(sums)
+    own_inv.wait()
+    own_div.wait()
     cross_first.wait_recv()
     ring_far[0].start()
     ring_far[1].start()
     ring_last[0].wait_recv()
+    ring_last[3].start()
+    cross_last[2].start()
+    ring_last[1].wait_recv()
     ring_last[2].start()
     cross_last[1].start()
-    ring_last[1].wait_recv()
-    ring_last[3].start()
-    cross_last[2].start()
-
     spread(0, (0,))
-
-    for part in range(2):
-        div_copies[part].wait_recv()
-        div_copies[5 + 2 * part].start()
-        div_copies[6 + 2 * part].start()
-    div_copies[4].start()
     ring_own[0].wait_recv()
+    ring_own[3].start()
+    ring_own[1].wait_recv()
     ring_own[2].start()
-    ring_own[1].wait_recv()
-    ring_own[3].start()
+    div_copies[0].wait_recv()
+    div_copies[5].start()
+    div_copies[6].start()
+    div_copies[1].wait_recv()
+    div_copies[7].start()
+    div_copies[8].start()
+    ring_last[2].wait_recv()
+    cross_last[3].start()
+    ring_last[3].wait_recv()
+    cross_last[4].start()
+    ring_far[0].wait_recv()
+    ring_far[3].start()
+    ring_far[1].wait_recv()
+    ring_far[2].start()
     for copy in meta_copies:
         copy.wait_recv()
     div_copies[2].wait_recv()
     div_copies[3].wait_recv()
-    spread(0, (1, 2))
-    ring_last[2].wait_recv()
-    cross_last[3].start()
-    ring_last[3].wait_recv()
-    cross_last[4].start()
+    spread(0, (1,2,))
     gather(0)
     product(0, 0)
-    ring_far[0].wait_recv()
-    ring_far[2].start()
-    ring_far[1].wait_recv()
-    ring_far[3].start()
     cross_last[0].wait_recv()
-    early = (1, 6, 2)
-    for rel in early:
-        gather(rel)
-        product(rel, 0)
-    for copy in div_copies[4:]:
-        copy.wait_recv()
-    spread(1, (0, 1, 2))
-    for rel in (0, *early):
-        product(rel, 1)
+    gather(1)
+    product(1, 0)
+    gather(2)
+    product(2, 0)
+    gather(6)
+    product(6, 0)
+    div_copies[4].wait_recv()
+    spread(1, (0,))
     ring_own[2].wait_recv()
     ring_own[3].wait_recv()
     gather(4)
     product(4, 0)
+    div_copies[5].wait_recv()
+    div_copies[6].wait_recv()
+    div_copies[7].wait_recv()
+    div_copies[8].wait_recv()
+    spread(1, (1,2,))
+    product(0, 1)
+    product(1, 1)
+    product(2, 1)
+    product(6, 1)
     product(4, 1)
-    for rel, copy in ((7, cross_last[1]), (3, cross_last[2])):
-        copy.wait_recv()
-        gather(rel)
-        product(rel, 0)
-        product(rel, 1)
-    for copy in (*cross_last[3:], *ring_far[2:]):
-        copy.wait_recv()
+    cross_last[2].wait_recv()
+    gather(3)
+    product(3, 0)
+    product(3, 1)
+    cross_last[1].wait_recv()
+    gather(7)
+    product(7, 0)
+    product(7, 1)
+    cross_last[3].wait_recv()
+    cross_last[4].wait_recv()
+    ring_far[2].wait_recv()
+    ring_far[3].wait_recv()
     gather(5)
     returns = [
         remote(

time: 67.4 us -> 65.8 us (0.976)
  the two profiles are of different devices: /device:TPU:24 before, /device:TPU:2 now
where the time goes in v4:
time: 65.8 us; the launch traced here: 65.6 us
  Pallas kernels  63.8 us (97%)
  local copies, waits for them, and re-layouts  1.87 us (3%)
    pallas_call x1, Pallas kernels, local(): pl.pallas_call(functools.partial(kernel, lon_count), out_shape=jax.ShapeD...  63.8 us
    unnamed x1, local copies, waits for them, and re-layouts  1.87 us

profile of v4, /device:TPU:2, one launch (start us, length us, event | category | flops | bytes accessed | tf_op | source)
XLA Modules:
  0.0 65.6 jit_solution(13321136735501230887)
XLA Ops:
  0.0 63.8 %shard_map.91 = f32[2,4,128,128]{3,2,1,0:T(8,128)} custom-call(s32[2,6]{1,0:T(2,128)} %owner_hbm.1, s32[2,6]{1,0:T(2,128)} %local_hbm.1, s32[2]{0:T(128)} %count_hbm.1, s32[2,5]{1,0:T(2,128)} %cols_hbm.1, s32[2]{0:T(128)} %inv_count_hbm.1, s32[2,4]{1,0:T(2,128)} %pattern_hbm.1, s32[2]{0:T(128)} %pattern_count_hbm.1, f32[12,128,128]{2,1,0:T(8,128)} %bitcast.2, ...), custom_call_target="tpu_custom_call" | custom-call | tf_op jit(solution)/shard_map/pallas_call | solution.py:456
  63.8 1.9 %copy.11 = f32[2,4,128,128]{3,2,1,0:T(8,128)} copy(f32[2,4,128,128]{3,2,1,0:T(8,128)} %shard_map.91) | data formatting | bytes 1048576

commit v5 on v4

--- a/solution.py
+++ b/solution.py
@@ -47,6 +47,7 @@
         given,
         packet,
         meta,
+        picks,
         owner_ref,
         local_ref,
         count_ref,
@@ -233,14 +234,13 @@
         for i, peer in enumerate(kin + near)
     ]
 
-    def spread(group, thirds):
+    def find(group):
         keys_own = own_key + 3 * group
-        home, beside = ((div_own, div_own_side), (div_mate, div_mate_side))[group]
 
         def one(rel, carry):
             owner_u = u + (rel % 2) * (SIDE - 1 - 2 * u)
             owner = at(owner_u, ring(rel // 2))
-            for third in thirds:
+            for third in range(3):
                 for p in range(rows):
                     base = p * slots_row
                     if third:
@@ -252,17 +252,32 @@
                         for l in range(slots_row):
                             hit = meta[keys_own + third, base + l] == wanted
                             second = jnp.where(hit, first, second)
-                            first = jnp.where(hit, l, first)
+                            first = jnp.where(hit, max(third - 1, 0) * listed + base + l, first)
+                        entry = ((third * rows + p) * vel_rows + c) * 2
+                        picks[group * CLASS + rel, entry] = first
+                        picks[group * CLASS + rel, entry + 1] = second
+            return carry
+
+        lax.fori_loop(0, CLASS, one, 0)
+
+    def spread(group, thirds):
+        home, beside = ((div_own, div_own_side), (div_mate, div_mate_side))[group]
+
+        def one(rel, carry):
+            place = group * CLASS + rel
+            for third in thirds:
+                source = beside if third else home
+                for p in range(rows):
+                    for c in range(vel_rows):
+                        entry = ((third * rows + p) * vel_rows + c) * 2
+                        first, second = picks[place, entry], picks[place, entry + 1]
                         one_on = jnp.where(first >= 0, 1.0, 0.0)
                         two_on = jnp.where(second >= 0, 1.0, 0.0)
-                        source = beside if third else home
-                        here = max(third - 1, 0) * listed + base
                         value = (
-                            one_on * source[here + jnp.maximum(first, 0)]
-                            + two_on * source[here + jnp.maximum(second, 0)]
+                            one_on * source[jnp.maximum(first, 0)]
+                            + two_on * source[jnp.maximum(second, 0)]
                         )
                         high, low = halves(value)
-                        place = group * CLASS + rel
                         lines = slice(p * side, (p + 1) * side)
                         at_high = slice(c * side, (c + 1) * side)
                         at_low = slice(width + c * side, width + (c + 1) * side)
@@ -317,19 +332,19 @@
             if only is not None:
                 only[p].start()
 
+    for copy in meta_copies:
+        copy.start()
     cross_first.start()
     ring_last[0].start()
     ring_last[1].start()
     ring_own[0].start()
     ring_own[1].start()
     cross_last[0].start()
-    div_copies[4].start()
+    div_copies[0].start()
+    div_copies[1].start()
     div_copies[2].start()
     div_copies[3].start()
-    div_copies[0].start()
-    div_copies[1].start()
-    for copy in meta_copies:
-        copy.start()
+    div_copies[4].start()
     sums[...] = jnp.zeros_like(sums)
     own_inv.wait()
     own_div.wait()
@@ -342,32 +357,34 @@
     ring_last[1].wait_recv()
     ring_last[2].start()
     cross_last[1].start()
-    spread(0, (0,))
+    for copy in meta_copies:
+        copy.wait_recv()
+    find(0)
+    div_copies[0].wait_recv()
+    div_copies[5].start()
+    div_copies[6].start()
     ring_own[0].wait_recv()
     ring_own[3].start()
     ring_own[1].wait_recv()
     ring_own[2].start()
-    div_copies[0].wait_recv()
-    div_copies[5].start()
-    div_copies[6].start()
     div_copies[1].wait_recv()
     div_copies[7].start()
     div_copies[8].start()
+    find(1)
+    spread(0, (0,))
     ring_last[2].wait_recv()
     cross_last[3].start()
     ring_last[3].wait_recv()
     cross_last[4].start()
-    ring_far[0].wait_recv()
-    ring_far[3].start()
-    ring_far[1].wait_recv()
-    ring_far[2].start()
-    for copy in meta_copies:
-        copy.wait_recv()
     div_copies[2].wait_recv()
     div_copies[3].wait_recv()
     spread(0, (1,2,))
     gather(0)
     product(0, 0)
+    ring_far[0].wait_recv()
+    ring_far[3].start()
+    ring_far[1].wait_recv()
+    ring_far[2].start()
     cross_last[0].wait_recv()
     gather(1)
     product(1, 0)
@@ -393,11 +410,9 @@
     product(4, 1)
     cross_last[2].wait_recv()
     gather(3)
-    product(3, 0)
     product(3, 1)
     cross_last[1].wait_recv()
     gather(7)
-    product(7, 0)
     product(7, 1)
     cross_last[3].wait_recv()
     cross_last[4].wait_recv()
@@ -415,6 +430,8 @@
         for p in range(rows)
     ]
     product(5, 1, returns)
+    product(3, 0)
+    product(7, 0)
     product(5, 0)
     for p in range(rows):
         returns[p].wait_recv()
@@ -471,6 +488,7 @@
             pltpu.VMEM((rows, side, width), F32),
             pltpu.SMEM((1, META_WIDTH), jnp.int32),
             pltpu.SMEM((CLASS + 6, META_WIDTH), jnp.int32),
+            pltpu.SMEM((2 * CLASS, 6 * rows * vel_rows), jnp.int32),
             *[pltpu.SMEM(value.shape, jnp.int32) for value in ints],
             pltpu.SemaphoreType.DMA((9,)),
             pltpu.SemaphoreType.DMA((9,)),

time: 65.8 us -> 64.5 us (0.980)
  Pallas kernels: 63.8 us -> 62.4 us
    pallas_call x1, Pallas kernels: 63.8 us -> 62.4 us  [local(): pl.pallas_call(functools.partial(kernel, lon_count), out_shape=jax.ShapeD...]
where the time goes in v5:
time: 64.5 us; the launch traced here: 64.3 us
  Pallas kernels  62.4 us (97%)
  local copies, waits for them, and re-layouts  1.87 us (3%)
    pallas_call x1, Pallas kernels, local(): pl.pallas_call(functools.partial(kernel, lon_count), out_shape=jax.ShapeD...  62.4 us
    unnamed x1, local copies, waits for them, and re-layouts  1.87 us

profile of v5, /device:TPU:2, one launch (start us, length us, event | category | flops | bytes accessed | tf_op | source)
XLA Modules:
  0.0 64.3 jit_solution(7805965705346470420)
XLA Ops:
  0.0 62.4 %shard_map.91 = f32[2,4,128,128]{3,2,1,0:T(8,128)} custom-call(s32[2,6]{1,0:T(2,128)} %owner_hbm.1, s32[2,6]{1,0:T(2,128)} %local_hbm.1, s32[2]{0:T(128)} %count_hbm.1, s32[2,5]{1,0:T(2,128)} %cols_hbm.1, s32[2]{0:T(128)} %inv_count_hbm.1, s32[2,4]{1,0:T(2,128)} %pattern_hbm.1, s32[2]{0:T(128)} %pattern_count_hbm.1, f32[12,128,128]{2,1,0:T(8,128)} %bitcast.2, ...), custom_call_target="tpu_custom_call" | custom-call | tf_op jit(solution)/shard_map/pallas_call | solution.py:473
  62.4 1.9 %copy.11 = f32[2,4,128,128]{3,2,1,0:T(8,128)} copy(f32[2,4,128,128]{3,2,1,0:T(8,128)} %shard_map.91) | data formatting | bytes 1048576

commit v6 on v5

--- a/solution.py
+++ b/solution.py
@@ -398,6 +398,10 @@
     ring_own[3].wait_recv()
     gather(4)
     product(4, 0)
+    cross_last[2].wait_recv()
+    gather(3)
+    cross_last[1].wait_recv()
+    gather(7)
     div_copies[5].wait_recv()
     div_copies[6].wait_recv()
     div_copies[7].wait_recv()
@@ -408,11 +412,7 @@
     product(2, 1)
     product(6, 1)
     product(4, 1)
-    cross_last[2].wait_recv()
-    gather(3)
     product(3, 1)
-    cross_last[1].wait_recv()
-    gather(7)
     product(7, 1)
     cross_last[3].wait_recv()
     cross_last[4].wait_recv()

time: 64.5 us -> 63.9 us (level)
  no operation moved by 1% of the time
where the time goes in v6:
time: 63.9 us; the launch traced here: 63.7 us
  Pallas kernels  61.9 us (97%)
  local copies, waits for them, and re-layouts  1.87 us (3%)
    pallas_call x1, Pallas kernels, local(): pl.pallas_call(functools.partial(kernel, lon_count), out_shape=jax.ShapeD...  61.9 us
    unnamed x1, local copies, waits for them, and re-layouts  1.87 us

profile of v6, /device:TPU:2, one launch (start us, length us, event | category | flops | bytes accessed | tf_op | source)
XLA Modules:
  0.0 63.7 jit_solution(6112951491406048442)
XLA Ops:
  0.0 61.9 %shard_map.91 = f32[2,4,128,128]{3,2,1,0:T(8,128)} custom-call(s32[2,6]{1,0:T(2,128)} %owner_hbm.1, s32[2,6]{1,0:T(2,128)} %local_hbm.1, s32[2]{0:T(128)} %count_hbm.1, s32[2,5]{1,0:T(2,128)} %cols_hbm.1, s32[2]{0:T(128)} %inv_count_hbm.1, s32[2,4]{1,0:T(2,128)} %pattern_hbm.1, s32[2]{0:T(128)} %pattern_count_hbm.1, f32[12,128,128]{2,1,0:T(8,128)} %bitcast.2, ...), custom_call_target="tpu_custom_call" | custom-call | tf_op jit(solution)/shard_map/pallas_call | solution.py:473
  61.9 1.9 %copy.11 = f32[2,4,128,128]{3,2,1,0:T(8,128)} copy(f32[2,4,128,128]{3,2,1,0:T(8,128)} %shard_map.91) | data formatting | bytes 1048576
